TPU v7x, 256 devices: a whole 4x4x8 slice. The times are simulated.
256 devices in a mesh: group: 8 (over x, core), dev: 32 (over y, z).
Axes of the slice: x: 4, y: 4, z: 8, core: 2. Of those that a mesh axis runs over, the one named last changes fastest.
Arguments:
- state: float32 [512, 5, 16, 256], P(('group', 'dev')), as said below
- new_owner: int32 [512], replicated, may hold values from 0 to 255, as said below
- neighbours: int32 [512, 6], replicated, may hold values from -1 to 511, as said below
Outputs:
- new_state: float32 [768, 5, 16, 256], P(('group', 'dev'))
Inputs may be any that keep to these rules, and one draw needn't show every extreme that they name: `new_owner`: owners never fall along the box order. Box m's new owner is its old owner m // 2 or the other device of the aligned pair (2 j, 2 j + 1) that holds it, so each device ends with 1 to 3 boxes, and some device holds exactly 3. `neighbours`: boxes sit at distinct points of an integer grid; an entry is -1 where no box is one step away across that face, else that box, always of the same group of 64 consecutive boxes; n is across face 2 a + 1 of m exactly when m is across face 2 a of n. `state`: density and pressure are positive in every cell.
All inputs are finite; a program needn't handle non-finite values.
Results may differ from a plain program's by a relative error of at most 0.0003.
Values sent between devices are 32-bit elements; how exact they have to be, the bound alone decides.
A program may use at most 64 MiB of HBM per device.

v0:
```python
import jax
import jax.numpy as jnp
from jax import lax
from jax.sharding import PartitionSpec as P

GAMMA = 1.4
COURANT = 0.3
FLIPPED = (1, 0, 3, 2, 5, 4)


def swapped(block, axis, apart):
    count = lax.axis_size(axis)
    route = []
    for low in range(count):
        high = low | 1 << apart
        if high != low and high < count:
            route += [(low, high), (high, low)]
    return lax.ppermute(block, axis, route)


def primitive(conserved):
    density = conserved[0]
    vel_x = conserved[1] / density
    vel_y = conserved[2] / density
    vel_z = conserved[3] / density
    pressure = (GAMMA - 1.0) * (
        conserved[4] - 0.5 * density * (vel_x * vel_x + vel_y * vel_y + vel_z * vel_z)
    )
    return (density, vel_x, vel_y, vel_z, pressure)


def minmod(lower, upper):
    return 0.5 * (jnp.sign(lower) + jnp.sign(upper)) * jnp.minimum(jnp.abs(lower), jnp.abs(upper))


def flux_parts(states, normal):
    density, vel_x, vel_y, vel_z, pressure = states
    normal_speed = (vel_x, vel_y, vel_z)[normal]
    energy = pressure / (GAMMA - 1.0) + 0.5 * density * (
        vel_x * vel_x + vel_y * vel_y + vel_z * vel_z
    )
    conserved = (density, density * vel_x, density * vel_y, density * vel_z, energy)
    fluxes = [item * normal_speed for item in conserved]
    fluxes[1 + normal] = fluxes[1 + normal] + pressure
    fluxes[4] = fluxes[4] + pressure * normal_speed
    sound = jnp.sqrt(GAMMA * pressure / density)
    return (conserved, fluxes, normal_speed, sound)


def hll(left, right, normal):
    cons_left, flux_left, speed_left, sound_left = flux_parts(left, normal)
    cons_right, flux_right, speed_right, sound_right = flux_parts(right, normal)
    slowest = jnp.minimum(jnp.minimum(speed_left - sound_left, speed_right - sound_right), 0.0)
    fastest = jnp.maximum(jnp.maximum(speed_left + sound_left, speed_right + sound_right), 0.0)
    spread = fastest - slowest
    return tuple(
        (
            (fastest * flux_a - slowest * flux_b + slowest * fastest * (cons_b - cons_a)) / spread
            for flux_a, flux_b, cons_a, cons_b in zip(flux_left, flux_right, cons_left, cons_right)
        )
    )


def fastest_signal(state):
    count, fields, edge, plane = state.shape
    flat = state.reshape(count, fields, edge * plane)
    density, vel_x, vel_y, vel_z, pressure = primitive(
        tuple((flat[:, index] for index in range(5)))
    )
    quickest = jnp.maximum(jnp.maximum(jnp.abs(vel_x), jnp.abs(vel_y)), jnp.abs(vel_z))
    return jnp.max(quickest + jnp.sqrt(GAMMA * pressure / density))


def exchange_boxes(blocks, parity):
    count = blocks.shape[0] - 1
    outgoing = lax.dynamic_slice_in_dim(blocks, 1 - parity, count, 0)
    return swapped(outgoing, "dev", 0)


def arrange(blocks, incoming, parity, owned, earlier, pair_start):
    boxes = blocks.shape[0]
    listing = jnp.concatenate([blocks, incoming], axis=0)
    slot_count = 2 * boxes - 1
    slot_index = jnp.arange(slot_count, dtype=jnp.int32)
    box_ids = earlier + slot_index
    offset = box_ids - pair_start
    odd_position = jnp.where(offset >= boxes, offset - boxes, boxes + offset - 1)
    position = jnp.clip(jnp.where(parity == 1, odd_position, offset), 0, slot_count - 1)
    placed = jnp.take(listing, position, axis=0)
    return (placed, jnp.where(slot_index < owned, box_ids, -1))


def face_layers(cube):
    count, fields, edge = (cube.shape[0], cube.shape[1], cube.shape[2])
    layers = []
    for axis in range(3):
        for side in range(2):
            begin = 0 if side == 0 else edge - 2
            layer = lax.slice_in_dim(cube, begin, begin + 2, axis=2 + axis)
            layers.append(layer.reshape(count, fields, 2 * edge * edge))
    return jnp.stack(layers, axis=1)


def fill_ghosts(cube, box_ids, neighbours):
    layers = face_layers(cube)
    wanted = jnp.where(
        box_ids[:, None] >= 0, jnp.take(neighbours, jnp.maximum(box_ids, 0), axis=0), -1
    )
    flipped = wanted[:, jnp.array(FLIPPED, dtype=jnp.int32)]
    piece_ids = lax.all_gather(box_ids, "dev", axis=0, tiled=True)
    piece_layers = lax.all_gather(layers, "dev", axis=0, tiled=True)
    match = ((flipped[:, :, None] == piece_ids[None, None, :]) & (flipped[:, :, None] >= 0)).astype(
        jnp.float32
    )
    ghosts = jnp.einsum("sgk,kgcx->sgcx", match, piece_layers, precision=lax.Precision.HIGHEST)
    return (ghosts, wanted)


def padded_boxes(cube, ghosts, wanted):
    count, fields, edge = (cube.shape[0], cube.shape[1], cube.shape[2])
    padded = jnp.pad(cube, ((0, 0), (0, 0), (2, 2), (2, 2), (2, 2)), mode="edge")
    for axis in range(3):
        for side in range(2):
            face = 2 * axis + side
            spots = [
                slice(None),
                slice(None),
                slice(2, 2 + edge),
                slice(2, 2 + edge),
                slice(2, 2 + edge),
            ]
            spots[2 + axis] = slice(0, 2) if side == 0 else slice(edge + 2, edge + 4)
            spots = tuple(spots)
            shape = [count, fields, edge, edge, edge]
            shape[2 + axis] = 2
            layer = ghosts[:, face ^ 1].reshape(shape)
            present = (wanted[:, face] >= 0)[:, None, None, None, None]
            padded = padded.at[spots].set(jnp.where(present, layer, padded[spots]))
    width = edge + 4
    return padded.reshape(count, fields, width * width * width)


def advance(flat, ratio, edge):
    count = flat.shape[0]
    width = edge + 4
    cells = width * width * width
    conserved = tuple((flat[:, index] for index in range(5)))
    states = primitive(conserved)
    parts = []
    for normal, stride in ((0, width * width), (1, width), (2, 1)):
        lefts = []
        rights = []
        for field in states:
            jumps = field[:, stride:] - field[:, : cells - stride]
            slope = minmod(jumps[:, : cells - 2 * stride], jumps[:, stride:])
            centre = field[:, stride : cells - stride]
            lefts.append((centre + 0.5 * slope)[:, : cells - 3 * stride])
            rights.append((centre - 0.5 * slope)[:, stride:])
        fluxes = hll(tuple(lefts), tuple(rights), normal)
        parts.append(
            tuple(
                (
                    jnp.pad(
                        flux[:, stride:] - flux[:, : cells - 4 * stride],
                        ((0, 0), (2 * stride, 2 * stride)),
                    )
                    for flux in fluxes
                )
            )
        )
    fields = []
    for index in range(5):
        total = parts[0][index] + parts[1][index] + parts[2][index]
        fresh = (conserved[index] - ratio * total).reshape(count, width, width, width)
        fresh = fresh[:, 2 : 2 + edge, 2 : 2 + edge, 2 : 2 + edge]
        fields.append(fresh.reshape(count, edge, edge * edge))
    return jnp.stack(fields, axis=1)


def body(state, new_owner, neighbours):
    boxes, fields, edge, plane = state.shape
    dev_count = lax.axis_size("dev")
    parity = lax.axis_index("dev") % 2
    place = lax.axis_index("group") * dev_count + lax.axis_index("dev")
    pair_start = (place - parity) * boxes
    owned = jnp.sum((new_owner == place).astype(jnp.int32))
    earlier = jnp.sum((new_owner < place).astype(jnp.int32))
    highest = lax.pmax(fastest_signal(state), ("group", "dev"))
    ratio = COURANT / highest
    incoming = exchange_boxes(state, parity)
    placed, slot_ids = arrange(state, incoming, parity, owned, earlier, pair_start)
    slot_count = placed.shape[0]
    live = (slot_ids >= 0)[:, None, None, None, None]
    cube = placed.reshape(slot_count, fields, edge, edge, edge)
    filler = jnp.array([1.0, 0.0, 0.0, 0.0, 2.5], jnp.float32)[None, :, None, None, None]
    cube = jnp.where(live, cube, filler)
    ghosts, wanted = fill_ghosts(cube, slot_ids, neighbours)
    fresh = advance(padded_boxes(cube, ghosts, wanted), ratio, edge)
    return jnp.where(slot_ids[:, None, None, None] >= 0, fresh, jnp.zeros_like(fresh))


def solution(mesh):
    placed = (P(("group", "dev"), None, None, None), P(), P())
    return jax.shard_map(
        body,
        mesh=mesh,
        in_specs=placed,
        out_specs=P(("group", "dev"), None, None, None),
        check_vma=False,
    )
```

profile of v0, /device:TPU:32, one launch (start us, length us, event | category | flops | bytes accessed | tf_op | source)
XLA Modules:
  0.0 526.7 jit_solution(5224151521216420585)
XLA Ops:
  6.5 0.9 constant_dynamic-slice_fusion
  7.4 1.8 collective-permute-start
  9.3 1.4 convert_reduce_fusion.1
  10.6 0.8 fusion.41
  11.4 1.3 maximum_compare_fusion
  12.7 0.6 compare_and_fusion
  13.3 0.9 pad_maximum_fusion.2
  14.3 0.6 gather_fusion
  14.9 1.9 gather.14
  16.7 1.9 select_select_fusion
  18.9 2.5 fusion.51
  22.4 6.1 %copy.99 = f32[3,5,16,16,2]{1,4,3,2,0:T(2,128)S(1)} copy(f32[3,5,16,16,2]{4,3,2,1,0:T(8,128)} %get-tuple-element.117) | data formatting | bytes 61440 | tf_op jit(solution)/shard_map/slice | solution.py:99
  28.9 6.1 %copy.100 = f32[3,5,16,16,2]{1,4,3,2,0:T(2,128)S(1)} copy(f32[3,5,16,16,2]{4,3,2,1,0:T(8,128)} %get-tuple-element.116) | data formatting | bytes 61440 | tf_op jit(solution)/shard_map/slice | solution.py:99
  35.5 0.8 copy.103
  36.4 0.8 add_reduce_fusion
  37.2 80.1 %pmax.7 = f32[]{:T(128)} all-reduce(f32[]{:T(128)} %add_reduce_fusion), channel_id=1, replica_groups=mesh['group'=8,'dev'=32] {'group','dev'}, use_global_device_ids=true, to_apply=%region_3.4 | all-reduce | flops 1 | bytes 8 | tf_op jit(solution)/shard_map/pmax | solution.py:188
  117.5 1.4 maximum_reduce_fusion
  118.9 0.6 gather_fusion.1
  119.6 0.6 dynamic-slice.54
  120.8 0.6 gather_fusion.2
  122.1 1.4 fusion.50
  123.4 17.4 %all-reduce.15 = s32[96]{0:T(128)S(1)} all-reduce(s32[96]{0:T(128)S(1)} %fusion.50), channel_id=1, replica_groups=mesh['group'=8,'dev'=32] {'dev'}, use_global_device_ids=true, to_apply=%add.15 | all-reduce | flops 96 | bytes 768
  141.7 0.8 pad_maximum_fusion
  142.5 2.9 slice_reduce_fusion.1
  145.4 1.0 reshape.456
  146.5 1.0 reshape.455
  147.5 7.2 %pad_maximum_fusion.1 = f32[3,5,20,20,20]{4,3,2,1,0:T(8,128)} fusion(f32[3,5,20,20,2]{4,3,2,1,0:T(8,128)S(1)} %reshape.456, f32[3,5,20,2,16]{4,3,2,1,0:T(2,128)S(1)} %reshape.454, f32[3,5,2,16,16]{4,3,2,1,0:T(8,128)S(1)} %reshape.452, f32[3,5,16,16,16]{4,3,2,1,0:T(8,128)S(1)} %select_select_fusion, f32[3,5,2,16,16]{4,3,2,1,0:T(8,128)S(1)} %reshape.451, ...), kind=kLoop, calls=%fused_computation.8 | loop fusion | flops 720000 | bytes 960000 | tf_op jit(solution)/shard_map/jit(_pad)/concatenate | solution.py:121
  154.7 9.2 %fusion.2 = f32[3,6,5,512]{3,0,2,1:T(4,128)S(1)} fusion(f32[96,6,5,512]{3,1,2,0:T(8,128)} %all-gather.2.cloned.1.call-done, s32[96]{0:T(128)S(1)} %all-reduce.15, s32[3,6]{0,1:T(8,128)S(1)} %bitcast.149, pred[3,6]{0,1:T(8,128)(4,1)S(1)} %broadcast_compare_fusion), kind=kOutput, calls=%fused_computation.12 | convolution fusion | flops 53087616 | bytes 6083034 | tf_op jit(solution)/shard_map/sgk,kgcx->sgcx/dot_general | solution.py:115
  164.7 10.2 %scatter.20 = f32[3,5,20,20,20]{4,3,2,1,0:T(8,128)} dynamic-update-slice(f32[3,5,20,20,20]{4,3,2,1,0:T(8,128)} %pad_maximum_fusion.1, f32[3,5,2,16,16]{4,3,2,1,0:T(8,128)S(1)} %copy_select_fusion, s32[]{:T(128)} %constant.296.clone.1, s32[]{:T(128)} %constant.296.clone.1, s32[]{:T(128)} %constant.296.clone.1, s32[]{:T(128)} %constant.299.clone.1, s32[]{:T(128)} %constant.299.clone.1) | dynamic-update-slice | bytes 61444 | tf_op jit(solution)/shard_map/scatter | solution.py:138
  174.9 1.1 slice_select_fusion.4
  176.0 10.2 %scatter.21 = f32[3,5,20,20,20]{4,3,2,1,0:T(8,128)} dynamic-update-slice(f32[3,5,20,20,20]{4,3,2,1,0:T(8,128)} %scatter.20, f32[3,5,2,16,16]{4,3,2,1,0:T(8,128)S(1)} %slice_select_fusion.4, s32[]{:T(128)} %constant.296.clone.1, s32[]{:T(128)} %constant.296.clone.1, s32[]{:T(128)} %constant.306.clone.1, s32[]{:T(128)} %constant.299.clone.1, s32[]{:T(128)} %constant.299.clone.1) | dynamic-update-slice | bytes 61444 | tf_op jit(solution)/shard_map/scatter | solution.py:138
  186.2 1.6 slice_select_fusion.3
  187.8 88.3 %scatter.24 = f32[3,5,20,20,20]{4,3,2,1,0:T(8,128)} dynamic-update-slice(f32[3,5,20,20,20]{4,3,2,1,0:T(8,128)} %scatter.21, f32[3,5,16,2,16]{4,3,2,1,0:T(2,128)S(1)} %slice_select_fusion.3, s32[]{:T(128)} %constant.296.clone.1, s32[]{:T(128)} %constant.296.clone.1, s32[]{:T(128)} %constant.299.clone.1, s32[]{:T(128)} %constant.296.clone.1, s32[]{:T(128)} %constant.299.clone.1) | dynamic-update-slice | bytes 61444 | tf_op jit(solution)/shard_map/scatter | solution.py:138
  276.5 1.6 slice_select_fusion.2
  278.0 88.1 %scatter.25 = f32[3,5,20,20,20]{4,3,2,1,0:T(8,128)} dynamic-update-slice(f32[3,5,20,20,20]{4,3,2,1,0:T(8,128)} %scatter.24, f32[3,5,16,2,16]{4,3,2,1,0:T(2,128)S(1)} %slice_select_fusion.2, s32[]{:T(128)} %constant.296.clone.1, s32[]{:T(128)} %constant.296.clone.1, s32[]{:T(128)} %constant.299.clone.1, s32[]{:T(128)} %constant.306.clone.1, s32[]{:T(128)} %constant.299.clone.1) | dynamic-update-slice | bytes 61444 | tf_op jit(solution)/shard_map/scatter | solution.py:138
  366.4 5.9 %copy.111 = f32[3,5,16,16,2]{4,3,2,1,0:T(8,128)S(1)} copy(f32[3,5,16,16,2]{1,4,3,2,0:T(2,128)S(1)} %bitcast.145) | data formatting | bytes 61440 | tf_op jit(solution)/shard_map/reshape;squeeze | solution.py:136
  372.3 3.5 slice_select_fusion.1
  375.8 25.4 %scatter.26 = f32[3,5,20,20,20]{4,3,2,1,0:T(8,128)} dynamic-update-slice(f32[3,5,20,20,20]{4,3,2,1,0:T(8,128)} %scatter.25, f32[3,5,16,16,2]{4,3,2,1,0:T(8,128)} %slice_select_fusion.1, s32[]{:T(128)} %constant.296.clone.1, s32[]{:T(128)} %constant.296.clone.1, s32[]{:T(128)} %constant.299.clone.1, s32[]{:T(128)} %constant.299.clone.1, s32[]{:T(128)} %constant.296.clone.1) | dynamic-update-slice | bytes 61444 | tf_op jit(solution)/shard_map/scatter | solution.py:138
  401.6 5.9 %copy.113 = f32[3,5,16,16,2]{4,3,2,1,0:T(8,128)S(1)} copy(f32[3,5,16,16,2]{1,4,3,2,0:T(2,128)S(1)} %bitcast.146) | data formatting | bytes 61440 | tf_op jit(solution)/shard_map/reshape;squeeze | solution.py:136
  407.5 3.7 slice_select_fusion
  411.2 84.7 %scatter.29 = f32[3,5,20,20,20]{4,3,2,1,0:T(8,128)} dynamic-update-slice(f32[3,5,20,20,20]{4,3,2,1,0:T(8,128)} %scatter.26, f32[3,5,16,16,2]{4,3,2,1,0:T(8,128)} %slice_select_fusion, s32[]{:T(128)} %constant.296.clone.1, s32[]{:T(128)} %constant.296.clone.1, s32[]{:T(128)} %constant.299.clone.1, s32[]{:T(128)} %constant.299.clone.1, s32[]{:T(128)} %constant.306.clone.1) | dynamic-update-slice | bytes 61444 | tf_op jit(solution)/shard_map/scatter | solution.py:138
  495.8 3.7 reshape.498
  505.3 0.8 fusion.16
  507.9 0.8 fusion.19
  508.8 0.5 add_divide_fusion.1
  510.5 0.7 fusion.26
  513.9 0.5 reshape.460
  518.9 0.8 broadcast_select_fusion
  (145 shorter events, 20.3 us)
Async XLA Ops:
  6.5 148.1 %all-gather.2.cloned.1.call-start = ((), (), s32[]{:S(2)}) async-start(), calls=%async_computation | async-start | bytes 8110080 | tf_op jit(solution)/shard_map/all_gather | solution.py:111
  7.4 5.9 %collective-permute-start = (f32[1,5,16,256]{3,2,1,0:T(8,128)S(1)}, f32[1,5,16,256]{3,2,1,0:T(8,128)S(1)}, u32[]{:S(2)}, u32[]{:S(2)}) collective-permute-start(f32[1,5,16,256]{3,2,1,0:T(8,128)S(1)} %constant_dynamic-slice_fusion), channel_id=1, source_target_pairs={{0,1},{1,0},{2,3},{3,2},{4,5},{5,4},{6,7},{7,6},{8,9},{9,8},{10,11... | collective-permute-start | bytes 245768 | tf_op jit(solution)/shard_map/ppermute | solution.py:18
  22.4 13.9 %copy-start = (f32[2,5,16,256]{3,2,1,0:T(8,128)S(1)}, f32[2,5,16,256]{3,2,1,0:T(8,128)}, u32[]{:S(2)}) copy-start(f32[2,5,16,256]{3,2,1,0:T(8,128)} %param.17) | copy-start | bytes 491524
  28.5 88.8 %copy-start.1 = (s32[512,6]{0,1:T(8,128)S(1)}, s32[512,6]{0,1:T(8,128)}, u32[]{:S(2)}) copy-start(s32[512,6]{0,1:T(8,128)} %param.19) | copy-start | bytes 36868
  28.5 91.1 %copy-start.3 = (u32[256]{0:T(256)S(1)}, u32[256]{0:T(256)}, u32[]{:S(2)}) copy-start(u32[256]{0:T(256)} %constant.355) | copy-start | bytes 3076
  28.6 92.2 %copy-start.2 = (s32[6]{0:T(128)S(1)}, s32[6]{0:T(128)}, u32[]{:S(2)}) copy-start(s32[6]{0:T(128)} %constant.352) | copy-start | bytes 76
Sparse Core Ops, SparseCore 0:
  36.4 97.1 all-gather.1
where the time goes:
time: 534 us; the launch traced here: 527 us
  local copies, waits for them, and re-layouts  358 us (67%)
  blocking collectives  97.5 us (18%)
  other arithmetic  44.1 us (8%)
  between operations  15.9 us (3%)
  matrix products  9.22 us (2%)
    scatter x6, local copies, waits for them, and re-layouts, padded_boxes(): padded = padded.at[spots].set(jnp.where(present, layer, padded[spots]))  307 us
    pmax x1, blocking collectives, body(): highest = lax.pmax(fastest_signal(state), ('group', 'dev'))  80.1 us
    unnamed x1, blocking collectives  17.4 us
    slice x5, local copies, waits for them, and re-layouts, face_layers(): layer = lax.slice_in_dim(cube, begin, begin + 2, axis=2 + axis)  15.1 us
    another operation x6, local copies, waits for them, and re-layouts, padded_boxes(): layer = ghosts[:, face ^ 1].reshape(shape)  12.8 us
    select_n x6, other arithmetic, padded_boxes(): padded = padded.at[spots].set(jnp.where(present, layer, padded[spots]))  11.5 us
  transfers between devices with their start and end apart: 2, of which 0 were waited for; matrix products, arithmetic and copies ran while one was open for 4% of the time, Pallas kernels for 0%

commit v1 on v0

v1 whole, which is shorter than its diff:
```python
import functools

import jax
import jax.numpy as jnp
from jax import lax
from jax.experimental import pallas as pl
from jax.experimental.pallas import tpu as pltpu
from jax.sharding import PartitionSpec as P

GAMMA = 1.4
COURANT = 0.3
MESH = pl.DeviceIdType.MESH
EDGE = 16
PLANE = 256
FIELDS = 5
FACES = 12
UNIT = 40
GROUPS = 8
DEVS = 32
ROWS_Y = 4
COLS_Z = 8


def primitive(conserved):
    density = conserved[0]
    vel_x = conserved[1] / density
    vel_y = conserved[2] / density
    vel_z = conserved[3] / density
    pressure = (GAMMA - 1.0) * (
        conserved[4] - 0.5 * density * (vel_x * vel_x + vel_y * vel_y + vel_z * vel_z)
    )
    return (density, vel_x, vel_y, vel_z, pressure)


def minmod(lower, upper):
    return jnp.maximum(jnp.minimum(lower, upper), 0.0) + jnp.minimum(jnp.maximum(lower, upper), 0.0)


def flux_parts(states, normal):
    density, vel_x, vel_y, vel_z, pressure = states
    normal_speed = (vel_x, vel_y, vel_z)[normal]
    energy = pressure * (1.0 / (GAMMA - 1.0)) + 0.5 * density * (
        vel_x * vel_x + vel_y * vel_y + vel_z * vel_z
    )
    conserved = (density, density * vel_x, density * vel_y, density * vel_z, energy)
    fluxes = [item * normal_speed for item in conserved]
    fluxes[1 + normal] = fluxes[1 + normal] + pressure
    fluxes[4] = fluxes[4] + pressure * normal_speed
    sound = jnp.sqrt(GAMMA * pressure / density)
    return (conserved, fluxes, normal_speed, sound)


def hll(left, right, normal):
    cons_left, flux_left, speed_left, sound_left = flux_parts(left, normal)
    cons_right, flux_right, speed_right, sound_right = flux_parts(right, normal)
    slowest = jnp.minimum(jnp.minimum(speed_left - sound_left, speed_right - sound_right), 0.0)
    fastest = jnp.maximum(jnp.maximum(speed_left + sound_left, speed_right + sound_right), 0.0)
    scale = 1.0 / (fastest - slowest)
    product = slowest * fastest
    return [
        (fastest * flux_a - slowest * flux_b + product * (cons_b - cons_a)) * scale
        for flux_a, flux_b, cons_a, cons_b in zip(flux_left, flux_right, cons_left, cons_right)
    ]


def swap_matrix(columns, pick):
    source = lax.broadcasted_iota(jnp.int32, (PLANE, columns), 0)
    lane = lax.broadcasted_iota(jnp.int32, (PLANE, columns), 1)
    wanted = (lane % EDGE) * EDGE + pick(lane // EDGE)
    return (source == wanted).astype(jnp.float32).astype(jnp.bfloat16)


def exact_permute(values, matrix):
    high = values.astype(jnp.bfloat16)
    rest = values - high.astype(jnp.float32)
    middle = rest.astype(jnp.bfloat16)
    low = (rest - middle.astype(jnp.float32)).astype(jnp.bfloat16)
    dot = functools.partial(jnp.dot, preferred_element_type=jnp.float32)
    return dot(high, matrix) + (dot(middle, matrix) + dot(low, matrix))


def lanes(rows):
    return lax.broadcasted_iota(jnp.int32, (rows, 128), 1)


def by_group(pieces, rows, begin):
    group = lanes(rows) // 32
    out = None
    for index, piece in enumerate(pieces):
        shift = (32 * index - begin) % 128
        moved = piece if shift == 0 else pltpu.roll(piece, shift, 1)
        out = moved if out is None else jnp.where(group == index, moved, out)
    return out


def pack_faces(x_ref, main_ref, extra_ref):
    half = lanes(8) < 64
    upper = lax.broadcasted_iota(jnp.int32, (8, 128), 0) < 4
    matrix = swap_matrix(128, lambda layer: jnp.where(layer < 2, layer, layer + 8))
    for box in range(2):
        cells = [x_ref[box, field] for field in range(FIELDS)]
        turned = exact_permute(jnp.concatenate(cells, axis=0), matrix)
        for side in range(2):
            first = 0 if side == 0 else EDGE - 2
            face = box * 6 + side
            for field in range(4):
                for layer in range(2):
                    for part in range(2):
                        row = 4 * field + 2 * layer + part
                        main_ref[face, row : row + 1, :] = x_ref[
                            box, field, first + layer : first + layer + 1, 128 * part : 128 * part + 128
                        ]
            for copy in range(2):
                for layer in range(2):
                    for part in range(2):
                        row = 4 * copy + 2 * layer + part
                        extra_ref[face, row : row + 1, :] = x_ref[
                            box, 4, first + layer : first + layer + 1, 128 * part : 128 * part + 128
                        ]
            twice = extra_ref[face]
            extra_ref[face] = jnp.where(half == upper, twice, pltpu.roll(twice, 64, 1))
            begin = 96 * side
            for axis in (1, 2):
                if axis == 1:
                    tiles = [cell[:, 128 * side : 128 * side + 128] for cell in cells]
                else:
                    tiles = [turned[EDGE * f : EDGE * f + EDGE] for f in range(FIELDS)]
                face = box * 6 + 2 * axis + side
                main_ref[face] = by_group(tiles[:4], EDGE, begin)
                last = tiles[4]
                extra_ref[face] = by_group([last[0:8], last[8:16]] * 2, 8, begin)
    main_ref[FACES] = jnp.zeros((EDGE, 128), jnp.float32)
    extra_ref[FACES] = jnp.zeros((8, 128), jnp.float32)


def local_signal(x_ref):
    best = None
    for box in range(2):
        density, vel_x, vel_y, vel_z, pressure = primitive([x_ref[box, f] for f in range(FIELDS)])
        quickest = jnp.maximum(jnp.maximum(jnp.abs(vel_x), jnp.abs(vel_y)), jnp.abs(vel_z))
        signal = quickest + jnp.sqrt(GAMMA * pressure / density)
        for row in range(2):
            for column in range(2):
                tile = signal[8 * row : 8 * row + 8, 128 * column : 128 * column + 128]
                best = tile if best is None else jnp.maximum(best, tile)
    return best


def share_kernel(base, table_ref, x_ref, got_ref, top_ref, main, extra, out, tops, ssem, rsem, tsem, usem):
    group = lax.axis_index("group")
    dev = lax.axis_index("dev")
    row, column = dev // COLS_Z, dev % COLS_Z
    barrier = pltpu.get_barrier_semaphore()

    def along_dev(step):
        return (group, lax.rem(dev + step, DEVS))

    stages = (
        (GROUPS, lambda step: (lax.rem(group + step, GROUPS), dev)),
        (ROWS_Y, lambda step: (group, lax.rem(row + step, ROWS_Y) * COLS_Z + column)),
        (COLS_Z, lambda step: (group, row * COLS_Z + lax.rem(column + step, COLS_Z))),
    )

    def greet(step, carry):
        pl.semaphore_signal(barrier, inc=1, device_id=along_dev(step), device_id_type=MESH)
        return carry

    lax.fori_loop(1, DEVS, greet, 0)
    if base == 0:
        for step in range(1, GROUPS):
            pl.semaphore_signal(barrier, inc=1, device_id=stages[0][1](step), device_id_type=MESH)
        tops[0, 0] = local_signal(x_ref)
    pack_faces(x_ref, main, extra)
    pl.semaphore_wait(barrier, DEVS - 1 + (GROUPS - 1 if base == 0 else 0))

    def small(stage, step):
        return pltpu.make_async_remote_copy(
            tops.at[stage, 0],
            tops.at[stage, step],
            tsem.at[stage, step],
            usem.at[stage, step],
            device_id=stages[stage][1](step),
            device_id_type=MESH,
        )

    def send_top(stage):
        for step in range(1, stages[stage][0]):
            small(stage, step).start()

    def take_top(stage):
        count = stages[stage][0]
        for step in range(1, count):
            small(stage, step).wait()
        best = tops[stage, 0]
        for step in range(1, count):
            best = jnp.maximum(best, tops[stage, step])
        return best

    def large(step):
        return pltpu.make_async_remote_copy(
            out.at[step],
            got_ref.at[step],
            ssem.at[step],
            rsem.at[step],
            device_id=along_dev(step),
            device_id_type=MESH,
        )

    half = lanes(8) < 64

    def fill(step, where):
        one = table_ref[4 * step + base]
        two = table_ref[4 * step + base + 1]
        where[step, 0:16, :] = main[one]
        where[step, 16:32, :] = main[two]
        where[step, 32:40, :] = jnp.where(half, extra[one], extra[two])

    def send(step, carry):
        fill(step, out)
        large(step).start()
        return carry

    if base == 0:
        send_top(0)
        lax.fori_loop(1, DEVS // 2, send, 0)
        tops[1, 0] = take_top(0)
        send_top(1)
        lax.fori_loop(DEVS // 2, DEVS, send, 0)
        fill(0, got_ref)
        tops[2, 0] = take_top(1)
        send_top(2)
        top_ref[...] = take_top(2)
    else:
        lax.fori_loop(1, DEVS, send, 0)
        fill(0, got_ref)
        top_ref[...] = jnp.zeros((8, 128), jnp.float32)

    def finish(step, carry):
        large(step).wait()
        return carry

    lax.fori_loop(1, DEVS, finish, 0)


def share(table, state, base):
    vmem = pl.BlockSpec(memory_space=pltpu.VMEM)
    return pl.pallas_call(
        functools.partial(share_kernel, base),
        out_shape=(
            jax.ShapeDtypeStruct((DEVS, UNIT, 128), jnp.float32),
            jax.ShapeDtypeStruct((8, 128), jnp.float32),
        ),
        in_specs=[pl.BlockSpec(memory_space=pltpu.SMEM), vmem],
        out_specs=(vmem, vmem),
        scratch_shapes=[
            pltpu.VMEM((FACES + 1, EDGE, 128), jnp.float32),
            pltpu.VMEM((FACES + 1, 8, 128), jnp.float32),
            pltpu.VMEM((DEVS, UNIT, 128), jnp.float32),
            pltpu.VMEM((3, 8, 8, 128), jnp.float32),
            pltpu.SemaphoreType.DMA((DEVS,)),
            pltpu.SemaphoreType.DMA((DEVS,)),
            pltpu.SemaphoreType.DMA((3, 8)),
            pltpu.SemaphoreType.DMA((3, 8)),
        ],
        compiler_params=pltpu.CompilerParams(
            collective_id=base, has_side_effects=True, vmem_limit_bytes=32 << 20
        ),
    )(table, state)


def rolled(arrays, amount, axis):
    return [pltpu.roll(a, amount % a.shape[axis], axis) for a in arrays]


def difference(states, normal, axis, unit):
    lefts, rights = [], []
    for field in states:
        (before,) = rolled([field], unit, axis)
        jump = field - before
        (after,) = rolled([jump], -unit, axis)
        half = 0.5 * minmod(jump, after)
        lefts.append(field + half)
        rights.append(field - half)
    fluxes = hll(rolled(lefts, unit, axis), rights, normal)
    return [high - low for high, low in zip(rolled(fluxes, -unit, axis), fluxes)]


def face_tile(ghosts, absent, present_low, present_high):
    lane = lanes(EDGE)
    low = jnp.where(present_low, ghosts[0], absent[0])
    high = jnp.where(present_high, ghosts[1], absent[1])
    return jnp.where(lane < 64, high, low)


def step_kernel(slots, where_ref, x_ref, got_ref, top_ref, out_ref, turned_ref, total_ref):
    ratio = COURANT / jnp.max(top_ref[...], axis=(0, 1), keepdims=True)
    matrix = swap_matrix(PLANE, lambda layer: layer)
    lane = lanes(EDGE)
    half = lanes(8) < 64
    row8 = lax.broadcasted_iota(jnp.int32, (8, PLANE), 0)

    def fetch(box, face):
        step = where_ref[box * 6 + face]
        slot = where_ref[FACES + box * 6 + face]
        present = where_ref[2 * FACES + box * 6 + face]
        begin = (slot // 2) * UNIT
        main = got_ref[step, pl.ds(pl.multiple_of(begin + (slot % 2) * 16, 8), 16), :]
        extra = got_ref[step, pl.ds(pl.multiple_of(begin + 32, 8), 8), :]
        extra = jnp.where(slot % 2 == 0, extra, pltpu.roll(extra, 64, 1))
        return main, extra, present > 0

    def lane_ghosts(main, extra, target):
        out = []
        for field in range(4):
            out.append(pltpu.roll(main, (target - 32 * field) % 128, 1))
        first = pltpu.roll(extra, target % 128, 1)
        second = pltpu.roll(extra, (target - 32) % 128, 1)
        out.append(jnp.concatenate([first, second], axis=0))
        return out

    def row_ghosts(main, extra):
        out = []
        last = jnp.where(half[0:4], extra[0:4], pltpu.roll(extra, 64, 1)[4:8])
        for field in range(FIELDS):
            rows = main[4 * field : 4 * field + 4] if field < 4 else last
            out.append(
                [
                    jnp.concatenate([rows[2 * layer : 2 * layer + 1], rows[2 * layer + 1 : 2 * layer + 2]], axis=1)
                    for layer in range(2)
                ]
            )
        return out

    def one_box(box, carry):
        cells = [x_ref[box, field] for field in range(FIELDS)]
        turned_ref[...] = exact_permute(jnp.concatenate(cells, axis=0), matrix)
        low_main, low_extra, low_there = fetch(box, 0)
        high_main, high_extra, high_there = fetch(box, 1)
        low = row_ghosts(low_main, low_extra)
        high = row_ghosts(high_main, high_extra)
        extended = []
        for field in range(FIELDS):
            edge_low = cells[field][0:1]
            edge_high = cells[field][EDGE - 1 : EDGE]
            l0 = jnp.where(low_there, low[field][0], edge_low)
            l1 = jnp.where(low_there, low[field][1], edge_low)
            h0 = jnp.where(high_there, high[field][0], edge_high)
            h1 = jnp.where(high_there, high[field][1], edge_high)
            tile = jnp.where(row8 == 0, h0, jnp.where(row8 == 7, l1, jnp.where(row8 == 6, l0, h1)))
            extended.append(jnp.concatenate([cells[field], tile], axis=0))
        for part in range(2):
            states = primitive([e[:, 128 * part : 128 * part + 128] for e in extended])
            parts = difference(states, 0, 0, 1)
            for field in range(FIELDS):
                total_ref[field, :, 128 * part : 128 * part + 128] = parts[field][0:EDGE]
        for axis in (2, 1):
            if axis == 1:
                source = cells
            else:
                source = [turned_ref[EDGE * f : EDGE * f + EDGE] for f in range(FIELDS)]
            low_main, low_extra, low_there = fetch(box, 2 * axis)
            high_main, high_extra, high_there = fetch(box, 2 * axis + 1)
            low = lane_ghosts(low_main, low_extra, 96)
            high = lane_ghosts(high_main, high_extra, 0)
            extended = []
            for field in range(FIELDS):
                left, right = source[field][:, 0:128], source[field][:, 128:256]
                edge_low = jnp.where(lane < 112, pltpu.roll(left, 96, 1), pltpu.roll(left, 112, 1))
                edge_high = jnp.where(lane < 16, pltpu.roll(right, 16, 1), pltpu.roll(right, 32, 1))
                tile = face_tile((low[field], high[field]), (edge_low, edge_high), low_there, high_there)
                extended.append(jnp.concatenate([left, right, tile], axis=1))
            pieces = []
            for part in range(2):
                states = primitive([e[8 * part : 8 * part + 8] for e in extended])
                pieces.append(difference(states, axis, 1, EDGE))
            if axis == 2:
                stacked = jnp.concatenate(
                    [pieces[part][f][:, 0:PLANE] for f in range(FIELDS) for part in range(2)], axis=0
                )
                turned_ref[...] = exact_permute(stacked, matrix)
            else:
                for field in range(FIELDS):
                    along = jnp.concatenate([pieces[part][field][:, 0:PLANE] for part in range(2)], axis=0)
                    total = (total_ref[field] + along) + turned_ref[EDGE * field : EDGE * field + EDGE]
                    out_ref[box, field] = cells[field] - ratio * total
        return carry

    lax.fori_loop(0, 2, one_box, 0)


def advance(where, state, got, top, slots):
    vmem = pl.BlockSpec(memory_space=pltpu.VMEM)
    return pl.pallas_call(
        functools.partial(step_kernel, slots),
        out_shape=jax.ShapeDtypeStruct(state.shape, state.dtype),
        in_specs=[pl.BlockSpec(memory_space=pltpu.SMEM), vmem, vmem, vmem],
        out_specs=vmem,
        scratch_shapes=[
            pltpu.VMEM((FIELDS * EDGE, PLANE), jnp.float32),
            pltpu.VMEM((FIELDS, EDGE, PLANE), jnp.float32),
        ],
        compiler_params=pltpu.CompilerParams(vmem_limit_bytes=32 << 20),
    )(where, state, got, top)


def tables(near, dev):
    face = jnp.arange(FACES, dtype=jnp.int32)
    there = near >= 0
    other = jnp.where(there, (near // 2) % DEVS, -1)
    same = (other[:, None] == other[None, :]) & there[:, None] & there[None, :]
    rank = jnp.sum((same & (face[None, :] < face[:, None])).astype(jnp.int32), axis=1)
    far_face = (near % 2) * 6 + ((face % 6) ^ 1)
    far_rank = jnp.sum((same & (far_face[None, :] < far_face[:, None])).astype(jnp.int32), axis=1)
    place = jnp.where(there, ((other - dev + DEVS) % DEVS) * 4 + rank, -1)
    spot = jnp.arange(4 * DEVS, dtype=jnp.int32)
    hit = spot[:, None] == place[None, :]
    table = FACES + jnp.sum(jnp.where(hit, face[None, :] - FACES, 0), axis=1)
    step = jnp.where(there, (dev - other + DEVS) % DEVS, 0)
    where = jnp.concatenate([step, jnp.where(there, far_rank, 0), there.astype(jnp.int32)])
    return table, where


def most_shared(neighbours):
    near = neighbours.reshape(-1, FACES)
    owner = jnp.where(near >= 0, near // 2, -1)
    same = (owner[:, :, None] == owner[:, None, :]) & (owner >= 0)[:, :, None]
    return jnp.max(jnp.sum(same.astype(jnp.int32), axis=2))


def body(state, new_owner, neighbours):
    group = lax.axis_index("group")
    dev = lax.axis_index("dev")
    place = group * DEVS + dev
    near = lax.dynamic_slice_in_dim(neighbours, 2 * place, 2, 0).reshape(FACES)
    table, where = tables(near, dev)
    got, top = share(table, state, 0)

    def few(state):
        return advance(where, state, got, top, 2)

    def many(state):
        more, _ = share(table, state, 2)
        return advance(where, state, jnp.concatenate([got, more], axis=1), top, 4)

    fresh = lax.cond(most_shared(neighbours) > 2, many, few, state)
    parity = dev % 2
    route = [(d, d ^ 1) for d in range(DEVS)]
    sent = lax.ppermute(jnp.where(parity == 0, fresh[1], fresh[0]), "dev", route)
    first = place // 2 * 4
    owners = lax.dynamic_slice_in_dim(new_owner, first, 4, 0)
    split = jnp.sum((owners == place // 2 * 2).astype(jnp.int32))
    none = jnp.zeros_like(sent)
    pick = lambda test, a, b: jnp.where(test, a, b)
    even = (fresh[0], pick(split >= 2, fresh[1], none), pick(split == 3, sent, none))
    odd = (
        pick(split == 1, sent, pick(split == 2, fresh[0], fresh[1])),
        pick(split == 1, fresh[0], pick(split == 2, fresh[1], none)),
        pick(split == 1, fresh[1], none),
    )
    return jnp.stack([pick(parity == 0, a, b) for a, b in zip(even, odd)])


def solution(mesh):
    placed = (P(("group", "dev"), None, None, None), P(), P())
    return jax.shard_map(
        body,
        mesh=mesh,
        in_specs=placed,
        out_specs=P(("group", "dev"), None, None, None),
        check_vma=False,
    )
```

time: 534 us -> 69.1 us (0.13); the launches traced: 527 us -> 68 us
  local copies, waits for them, and re-layouts: 358 us -> 4.54 us
  blocking collectives: 97.5 us -> 0 us
  Pallas kernels: 0 us -> 55.1 us
  other arithmetic: 44.1 us -> 4.4 us
  between operations: 15.9 us -> 3.24 us
  matrix products: 9.22 us -> 0 us
    scatter x6 -> x0, local copies, waits for them, and re-layouts: 307 us -> none  [padded_boxes(): padded = padded.at[spots].set(jnp.where(present, layer, padded[spots]))]
    pmax x1 -> x0, blocking collectives: 80.1 us -> none  [body(): highest = lax.pmax(fastest_signal(state), ('group', 'dev'))]
    pallas_call x0 -> x3, Pallas kernels: none -> 55.1 us  [the longest x2 52 us: share(): pl.pallas_call(functools.partial(share_kernel, base), out_shape=(jax.Shap...]
    slice x33 -> x1, local copies, waits for them, and re-layouts: 21.7 us -> 0.66 us  [body(): fresh[1]]
    unnamed x1 -> x0, blocking collectives: 17.4 us -> none
    another operation x20 -> x0, local copies, waits for them, and re-layouts: 16.1 us -> none  [the longest x6 12.8 us: padded_boxes(): layer = ghosts[:, face ^ 1].reshape(shape)]
    select_n x10 -> x4, other arithmetic: 15 us -> 1.01 us  [the longest x1 0.95 us: body(): pick = lambda test, a, b: jnp.where(test, a, b)]
    dot_general x1 -> x0, matrix products: 9.22 us -> none  [fill_ghosts(): jnp.einsum('sgk,kgcx->sgcx', match, piece_layers, precision=lax.Precision...]
  transfers between devices with their start and end apart: 2 -> 1, of which waited for: 0 -> 0; matrix products, arithmetic and copies ran while one was open for 4% -> 3% of each run, Pallas kernels for 0% -> 0%
where the time goes in v1:
time: 69.1 us; the launch traced here: 68 us
  Pallas kernels  55.1 us (80%)
  local copies, waits for them, and re-layouts  4.54 us (7%)
  other arithmetic  4.4 us (6%)
  between operations  3.24 us (5%)
  starting transfers between devices  0.7 us (1%)
    pallas_call x2, Pallas kernels, share(): pl.pallas_call(functools.partial(share_kernel, base), out_shape=(jax.Shap...  52 us
    pallas_call x1, Pallas kernels, advance(): pl.pallas_call(functools.partial(step_kernel, slots), out_shape=jax.Shape...  3.1 us
    cond x2, local copies, waits for them, and re-layouts  1.77 us
    reduce_sum x1, other arithmetic, body(): split = jnp.sum((owners == place // 2 * 2).astype(jnp.int32))  1.4 us
  transfers between devices with their start and end apart: 1, of which 0 were waited for; matrix products, arithmetic and copies ran while one was open for 3% of the time, Pallas kernels for 0%

profile of v1, /device:TPU:32, one launch (start us, length us, event | category | flops | bytes accessed | tf_op | source)
XLA Modules:
  0.0 68.0 jit_solution(3968317891626671125)
XLA Ops:
  0.0 0.0 copy-start
  0.0 0.8 %constant_dynamic-slice_fusion = s32[2,6]{0,1:T(8,128)S(1)} fusion(s32[512,6]{0,1:T(8,128)} %param.7, s32[]{:T(128)S(6)} %select_n.220), kind=kLoop, calls=%fused_computation.56 | loop fusion | bytes 100 | tf_op jit(solution)/shard_map/dynamic_slice | solution.py:434
  0.8 0.1 copy.11
  0.9 0.1 reshape.279
  1.0 0.2 convert_reduce_fusion.1
  1.2 0.1 select_reduce_fusion
  1.3 28.0 %shard_map.37 = (f32[32,40,128]{2,1,0:T(8,128)S(1)}, f32[8,128]{1,0:T(8,128)S(1)}) custom-call(s32[128]{0:T(128)S(1)} %broadcast_add_fusion.table_ref, f32[2,5,16,256]{3,2,1,0:T(8,128)} %x_ref.1), custom_call_target="tpu_custom_call" | custom-call | tf_op jit(solution)/shard_map/pallas_call | solution.py:247
  29.3 0.1 pad_add_fusion
  29.4 0.9 %copy.7 = s32[512,6]{1,0:T(8,128)S(1)} copy(s32[512,6]{0,1:T(8,128)} %param.7) | data formatting | bytes 24576 | tf_op args[2]
  30.3 0.1 reshape.278
  30.4 0.1 broadcast_compare_fusion
  30.5 0.1 copy.8
  30.6 0.1 copy.10
  30.7 0.1 convert_reduce_fusion
  30.8 0.6 reduce_max.9
  32.1 0.0 copy-done
  32.1 29.6 %conditional.1 = (f32[1,5,16,256]{3,2,1,0:T(8,128)}, f32[1,5,16,256]{3,2,1,0:T(8,128)}, f32[5,16,256]{2,1,0:T(8,128)S(1)}, f32[5,16,256]{2,1,0:T(8,128)S(1)}) conditional(s32[]{:T(128)} %convert_element_type.19, (s32[36]{0:T(128)S(1)}, f32[2,5,16,256]{3,2,1,0:T(8,128)S(1)}, f32[32,40,128]{2,1,0:T(8,128)S(1)}, f32[8,128]{1,0:T(8,128)S(1)}) %tuple.33, ...), branch_computations={%region_5.6_spmd, %region_6.7_spmd} | conditional | flops 327680 | bytes 3276832 | solution.py:445
  32.1 24.0 %branch_1_fun.4 = (f32[32,40,128]{2,1,0:T(8,128)S(1)}, f32[8,128]{1,0:T(8,128)}) custom-call(s32[128]{0:T(128)S(1)} %get-tuple-element.44.table_ref, f32[2,5,16,256]{3,2,1,0:T(8,128)S(1)} %get-tuple-element.42.x_ref), custom_call_target="tpu_custom_call" | custom-call | tf_op jit(solution)/shard_map/cond/branch_1_fun/pallas_call | solution.py:247
  56.0 0.1 pad_maximum_fusion.got_ref
  56.1 3.1 %branch_1_fun.5 = f32[2,5,16,256]{3,2,1,0:T(8,128)S(1)} custom-call(s32[36]{0:T(128)S(1)} %get-tuple-element.41.where_ref, f32[2,5,16,256]{3,2,1,0:T(8,128)S(1)} %get-tuple-element.42.x_ref, f32[32,80,128]{2,1,0:T(8,128)S(1)} %pad_maximum_fusion.got_ref, f32[8,128]{1,0:T(8,128)S(1)} %get-tuple-element.46.top_ref), custom_call_target="tpu_custom_call" | custom-call | tf_op jit(solution)/shard_map/cond/branch_1_fun/pallas_call | solution.py:393
  59.3 0.7 fusion.20
  59.9 0.9 %copy.18 = f32[5,16,256]{2,1,0:T(8,128)S(1)} copy(f32[5,16,256]{2,1,0:T(8,128)} %bitcast.2) | data formatting | bytes 163840 | tf_op jit(solution)/shard_map/cond
  60.8 0.9 %copy.19 = f32[5,16,256]{2,1,0:T(8,128)S(1)} copy(f32[5,16,256]{2,1,0:T(8,128)} %bitcast.3) | data formatting | bytes 163840 | tf_op jit(solution)/shard_map/cond
  61.7 0.7 %collective-permute-start = (f32[5,16,256]{2,1,0:T(8,128)S(1)}, f32[5,16,256]{2,1,0:T(8,128)S(1)}, u32[]{:S(2)}, u32[]{:S(2)}) collective-permute-start(f32[5,16,256]{2,1,0:T(8,128)S(1)} %broadcast_select_fusion), channel_id=1, source_target_pairs={{0,1},{1,0},{2,3},{3,2},{4,5},{5,4},{6,7},{7,6},{8,9},{9,8},{10,11... | collective-permute-start | bytes 245768 | tf_op jit(solution)/shard_map/ppermute | solution.py:448
  62.4 1.4 %fusion.12 = s32[]{:T(128)} fusion(s32[512]{0:T(512)} %param.6, s32[]{:T(128)S(6)} %select_n.233, s32[]{:T(128)S(6)} %mul.35), kind=kLoop, calls=%fused_computation.47 | loop fusion | flops 11 | bytes 28 | tf_op jit(solution)/shard_map/reduce_sum | solution.py:451
  65.7 0.9 %select_select_fusion = f32[1,5,16,256]{3,2,1,0:T(8,128)S(1)} fusion(f32[1,5,16,256]{3,2,1,0:T(8,128)} %get-tuple-element.58, f32[1,5,16,256]{3,2,1,0:T(8,128)} %get-tuple-element.57, pred[]{:T(512)S(6)} %eq.84, pred[]{:T(512)S(6)} %eq.83, pred[]{:T(512)S(6)} %ge.47, pred[]{:T(512)S(6)} %eq.71), kind=kLoop, calls=%fused_computation.12 | loop fusion | flops 81920 | bytes 245764 | tf_op jit(solution)/shard_map/jit(_where)/select_n | solution.py:453
  67.2 0.0 collective-permute-done
  67.3 0.7 %pad_maximum_fusion.1 = f32[3,5,16,256]{3,2,1,0:T(8,128)} fusion(f32[1,5,16,256]{3,2,1,0:T(8,128)S(1)} %get-tuple-element.70, f32[1,5,16,256]{3,2,1,0:T(8,128)S(1)} %select_select_fusion, f32[1,5,16,256]{3,2,1,0:T(8,128)S(1)} %get-tuple-element.69), kind=kLoop, calls=%fused_computation.1 | loop fusion | flops 122880 | bytes 491520 | tf_op jit(solution)/shard_map/stack | solution.py:460
  (6 shorter events, 0.1 us)
Async XLA Ops:
  0.0 32.1 %copy-start = (f32[2,5,16,256]{3,2,1,0:T(8,128)S(1)}, f32[2,5,16,256]{3,2,1,0:T(8,128)}, u32[]{:S(2)}) copy-start(f32[2,5,16,256]{3,2,1,0:T(8,128)} %x_ref.1) | copy-start | bytes 491524
  61.7 5.5 %collective-permute-start = (f32[5,16,256]{2,1,0:T(8,128)S(1)}, f32[5,16,256]{2,1,0:T(8,128)S(1)}, u32[]{:S(2)}, u32[]{:S(2)}) collective-permute-start(f32[5,16,256]{2,1,0:T(8,128)S(1)} %broadcast_select_fusion), channel_id=1, source_target_pairs={{0,1},{1,0},{2,3},{3,2},{4,5},{5,4},{6,7},{7,6},{8,9},{9,8},{10,11... | collective-permute-start | bytes 245768 | tf_op jit(solution)/shard_map/ppermute | solution.py:448

commit v2 on v1

v2 whole, which is shorter than its diff:
```python
import functools

import jax
import jax.numpy as jnp
from jax import lax
from jax.experimental import pallas as pl
from jax.experimental.pallas import tpu as pltpu
from jax.sharding import PartitionSpec as P

GAMMA = 1.4
COURANT = 0.3
MESH = pl.DeviceIdType.MESH
EDGE = 16
PLANE = 256
FIELDS = 5
FACES = 12
UNIT = 5
RECORD = 3
OWN = (FACES + 1) * RECORD
CAP_Z = 5
CAP_Y = 6
CAP_HERE = 12


def unit_tiles(cap):
    return 2 * cap + (cap + 1) // 2


UNIT_Z = unit_tiles(CAP_Z)
UNIT_Y = unit_tiles(CAP_Y)
HERE = 3 * UNIT_Y
GROUPS = 8
DEVS = 32
ROWS_Y = 4
COLS_Z = 8


def primitive(conserved):
    density = conserved[0]
    vel_x = conserved[1] / density
    vel_y = conserved[2] / density
    vel_z = conserved[3] / density
    pressure = (GAMMA - 1.0) * (
        conserved[4] - 0.5 * density * (vel_x * vel_x + vel_y * vel_y + vel_z * vel_z)
    )
    return (density, vel_x, vel_y, vel_z, pressure)


def minmod(lower, upper):
    return jnp.maximum(jnp.minimum(lower, upper), 0.0) + jnp.minimum(jnp.maximum(lower, upper), 0.0)


def flux_parts(states, normal):
    density, vel_x, vel_y, vel_z, pressure = states
    normal_speed = (vel_x, vel_y, vel_z)[normal]
    energy = pressure * (1.0 / (GAMMA - 1.0)) + 0.5 * density * (
        vel_x * vel_x + vel_y * vel_y + vel_z * vel_z
    )
    conserved = (density, density * vel_x, density * vel_y, density * vel_z, energy)
    fluxes = [item * normal_speed for item in conserved]
    fluxes[1 + normal] = fluxes[1 + normal] + pressure
    fluxes[4] = fluxes[4] + pressure * normal_speed
    sound = jnp.sqrt(GAMMA * pressure / density)
    return (conserved, fluxes, normal_speed, sound)


def hll(left, right, normal):
    cons_left, flux_left, speed_left, sound_left = flux_parts(left, normal)
    cons_right, flux_right, speed_right, sound_right = flux_parts(right, normal)
    slowest = jnp.minimum(jnp.minimum(speed_left - sound_left, speed_right - sound_right), 0.0)
    fastest = jnp.maximum(jnp.maximum(speed_left + sound_left, speed_right + sound_right), 0.0)
    scale = 1.0 / (fastest - slowest)
    product = slowest * fastest
    return [
        (fastest * flux_a - slowest * flux_b + product * (cons_b - cons_a)) * scale
        for flux_a, flux_b, cons_a, cons_b in zip(flux_left, flux_right, cons_left, cons_right)
    ]


def swap_matrix(columns, pick):
    source = lax.broadcasted_iota(jnp.int32, (PLANE, columns), 0)
    lane = lax.broadcasted_iota(jnp.int32, (PLANE, columns), 1)
    wanted = (lane % EDGE) * EDGE + pick(lane // EDGE)
    return (source == wanted).astype(jnp.float32).astype(jnp.bfloat16)


def exact_permute(values, matrix):
    high = values.astype(jnp.bfloat16)
    rest = values - high.astype(jnp.float32)
    middle = rest.astype(jnp.bfloat16)
    low = (rest - middle.astype(jnp.float32)).astype(jnp.bfloat16)
    dot = functools.partial(jnp.dot, preferred_element_type=jnp.float32)
    return dot(high, matrix) + (dot(middle, matrix) + dot(low, matrix))


def lanes(rows):
    return lax.broadcasted_iota(jnp.int32, (rows, 128), 1)


def by_group(pieces, rows, begin):
    group = lanes(rows) // 32
    out = None
    for index, piece in enumerate(pieces):
        shift = (32 * index - begin) % 128
        moved = piece if shift == 0 else pltpu.roll(piece, shift, 1)
        out = moved if out is None else jnp.where(group == index, moved, out)
    return out


def pack_faces(x_ref, pool):
    half = lanes(8) < 64
    upper = lax.broadcasted_iota(jnp.int32, (8, 128), 0) < 4
    matrix = swap_matrix(128, lambda layer: jnp.where(layer < 2, layer, layer + 8))
    for box in range(2):
        cells = [x_ref[box, field] for field in range(FIELDS)]
        turned = exact_permute(jnp.concatenate(cells, axis=0), matrix)
        for side in range(2):
            first = 0 if side == 0 else EDGE - 2
            begin = RECORD * (box * 6 + side)
            for place in range(24):
                field, layer, part = min(place // 4, 4), place // 2 % 2, place % 2
                pool[begin + place // 8, place % 8 : place % 8 + 1, :] = x_ref[
                    box, field, first + layer : first + layer + 1, 128 * part : 128 * part + 128
                ]
            twice = pool[begin + 2]
            pool[begin + 2] = jnp.where(half == upper, twice, pltpu.roll(twice, 64, 1))
            source = 96 * side
            for axis in (1, 2):
                if axis == 1:
                    tiles = [cell[:, 128 * side : 128 * side + 128] for cell in cells]
                else:
                    tiles = [turned[EDGE * f : EDGE * f + EDGE] for f in range(FIELDS)]
                begin = RECORD * (box * 6 + 2 * axis + side)
                main = by_group(tiles[:4], EDGE, source)
                pool[begin] = main[0:8]
                pool[begin + 1] = main[8:16]
                last = tiles[4]
                pool[begin + 2] = by_group([last[0:8], last[8:16]] * 2, 8, source)
    for tile in range(RECORD * FACES, OWN):
        pool[tile] = jnp.zeros((8, 128), jnp.float32)


def local_signal(x_ref):
    best = None
    for box in range(2):
        density, vel_x, vel_y, vel_z, pressure = primitive([x_ref[box, f] for f in range(FIELDS)])
        quickest = jnp.maximum(jnp.maximum(jnp.abs(vel_x), jnp.abs(vel_y)), jnp.abs(vel_z))
        signal = quickest + jnp.sqrt(GAMMA * pressure / density)
        for row in range(2):
            for column in range(2):
                tile = signal[8 * row : 8 * row + 8, 128 * column : 128 * column + 128]
                best = tile if best is None else jnp.maximum(best, tile)
    return best


def fill_tables(near_ref, row, column, tab):
    square = (128, 128)
    index = lax.broadcasted_iota(jnp.int32, square, 0)
    lane = lax.broadcasted_iota(jnp.int32, square, 1)
    spread = (
        lax.broadcasted_iota(jnp.int32, (6, 128), 1) % 8 == lax.broadcasted_iota(jnp.int32, (6, 128), 0)
    ).astype(jnp.float32)
    tiled = jnp.dot(
        near_ref[...].astype(jnp.float32), spread, precision=lax.Precision.HIGHEST, preferred_element_type=jnp.float32
    )
    here = lanes(16) // 8 == lax.broadcasted_iota(jnp.int32, (16, 128), 0)
    flat = jnp.sum(jnp.where(here, tiled, 0.0), axis=0, keepdims=True)
    across = jnp.broadcast_to(flat, square)
    down = jnp.transpose(across)

    def facts(values, q):
        near = values.astype(jnp.int32)
        there = (near >= 0) & (q % 8 < 6)
        other = (near // 2) % DEVS
        far_row, far_column = other // COLS_Z, other % COLS_Z
        far_face = (near % 2) * 6 + (q % 8) + 1 - 2 * (q % 2)
        return there, far_row, far_column, far_face

    there, far_row, far_column, far_face = facts(down, index)
    there_j, far_row_j, far_column_j, far_face_j = facts(across, lane)
    ones = jnp.ones(square, jnp.bfloat16)

    def rank(test):
        hits = jnp.where(test, 1.0, 0.0).astype(jnp.bfloat16)
        return jnp.dot(hits, ones, preferred_element_type=jnp.float32).astype(jnp.int32)

    source = index // 16
    own = there & (source == column)
    before = (source == lane // 16) & (lane < index) & there_j
    rank_z = rank(before & (far_column_j == far_column))
    rank_here = rank(before & (far_row_j == far_row))
    held = there & (far_column == column)
    held_j = there_j & (far_column_j == column)
    rank_y = rank(held_j & (far_row_j == far_row) & (far_face_j < far_face))

    def total(test, values):
        return jnp.sum(jnp.where(test, values, 0), axis=0, keepdims=True)

    face = (index // 8 % 2) * 6 + index % 8
    step = (far_column - column + COLS_Z) % COLS_Z
    fits = own & (step > 0) & (rank_z < CAP_Z)
    hit = fits & (step * CAP_Z + rank_z == lane)
    tab[0:1, :] = RECORD * FACES + total(hit, RECORD * (face - FACES))
    over = own & (step > 0) & (rank_z >= CAP_Z)
    back = (column - source + COLS_Z) % COLS_Z
    begin = OWN + (back - 1) * UNIT_Z
    main = jnp.where(back == 0, RECORD * face, begin + 2 * rank_z)
    last = jnp.where(back == 0, RECORD * face + 2, begin + 2 * CAP_Z + rank_z // 2)
    side = jnp.where(back == 0, 0, rank_z % 2)
    step = (far_row - row + ROWS_Y) % ROWS_Y
    near_by = step == 0
    base = jnp.where(near_by, 3 * CAP_Y, (step - 1) * CAP_Y)
    fits = held & (near_by | (rank_y < CAP_Y))
    hit = fits & (base + rank_y == lane)
    tab[1:2, :] = RECORD * FACES + total(hit, main - RECORD * FACES)
    tab[2:3, :] = RECORD * FACES + 2 + total(hit, last - RECORD * FACES - 2)
    tab[3:4, :] = total(hit, side)
    step = (row - far_row + ROWS_Y) % ROWS_Y
    near_by = step == 0
    over = over | (own & ~near_by & (rank_here >= CAP_Y))
    begin = jnp.where(near_by, HERE, (step - 1) * UNIT_Y)
    cap = jnp.where(near_by, CAP_HERE, CAP_Y)
    hit = own & (near_by | (rank_here < CAP_Y)) & (face == lane)
    tab[4:5, :] = total(hit, begin + 2 * rank_here)
    tab[5:6, :] = total(hit, begin + 2 * cap + rank_here // 2)
    tab[6:7, :] = total(hit, rank_here % 2)
    tab[7:8, :] = total(hit, 1)
    return jnp.max(jnp.where(over, 1.0, 0.0), axis=0, keepdims=True)


def move_records(pool, entries, target, start):
    half = lanes(8) < 64
    cap = len(entries)
    for index, (main, _, _) in enumerate(entries):
        target[start + 2 * index] = pool[main]
        target[start + 2 * index + 1] = pool[main + 1]

    def last(entry, wanted):
        tile = pool[entry[1]]
        if entry[2] is None:
            return tile
        side = jnp.full((8, 128), entry[2], jnp.int32)
        return jnp.where(side == wanted, tile, pltpu.roll(tile, 64, 1))

    for pair in range((cap + 1) // 2):
        tile = last(entries[2 * pair], 0)
        if 2 * pair + 1 < cap:
            tile = jnp.where(half, tile, last(entries[2 * pair + 1], 1))
        target[start + 2 * cap + pair] = tile


def share_kernel(
    x_hbm, near_hbm, got_ref, top_ref, tab_ref, x_ref, near_ref, tab, own, pool, out_z, out_y, tops,
    insem, zsend, zgot, ysend, ygot, tsend, tgot,
):
    group = lax.axis_index("group")
    dev = lax.axis_index("dev")
    row, column = dev // COLS_Z, dev % COLS_Z
    start = pl.multiple_of((group * ROWS_Y + row) * 2 * COLS_Z, 16)
    load_near = pltpu.make_async_copy(near_hbm.at[pl.ds(start, 2 * COLS_Z), :], near_ref, insem.at[0])
    load_x = pltpu.make_async_copy(x_hbm, x_ref, insem.at[1])
    load_tab = pltpu.make_async_copy(tab_ref, tab, insem.at[2])
    load_near.start()
    load_x.start()
    barrier = pltpu.get_barrier_semaphore()

    def z_peer(step):
        return (group, row * COLS_Z + lax.rem(column + step, COLS_Z))

    def y_peer(step):
        return (group, lax.rem(row + step, ROWS_Y) * COLS_Z + column)

    def group_peer(step):
        return (lax.rem(group + step, GROUPS), dev)

    stages = ((COLS_Z, z_peer), (ROWS_Y, y_peer), (GROUPS, group_peer))
    for count, peer in stages:
        for step in range(1, count):
            pl.semaphore_signal(barrier, inc=1, device_id=peer(step), device_id_type=MESH)
    load_near.wait()
    over = fill_tables(near_ref, row, column, tab_ref)
    load_tab.start()
    load_x.wait()
    tops[0, 0, 0:1] = jnp.max(local_signal(x_ref), axis=0, keepdims=True)
    tops[0, 0, 1:2] = over
    pack_faces(x_ref, own)
    load_tab.wait()
    pl.semaphore_wait(barrier, COLS_Z + ROWS_Y + GROUPS - 3)

    def small(stage, step):
        return pltpu.make_async_remote_copy(
            tops.at[stage, 0],
            tops.at[stage, step],
            tsend.at[stage, step],
            tgot.at[stage, step],
            device_id=stages[stage][1](step),
            device_id_type=MESH,
        )

    def send_top(stage):
        for step in range(1, stages[stage][0]):
            small(stage, step).start()

    def take_top(stage):
        count = stages[stage][0]
        for step in range(1, count):
            small(stage, step).wait()
        best = tops[stage, 0]
        for step in range(1, count):
            best = jnp.maximum(best, tops[stage, step])
        return best

    def z_copy(step):
        return pltpu.make_async_remote_copy(
            out_z.at[step],
            pool.at[pl.ds(OWN + (step - 1) * UNIT_Z, UNIT_Z)],
            zsend.at[step],
            zgot.at[step],
            device_id=z_peer(step),
            device_id_type=MESH,
        )

    def y_copy(step):
        return pltpu.make_async_remote_copy(
            out_y.at[step],
            got_ref.at[pl.ds((step - 1) * UNIT_Y, UNIT_Y)],
            ysend.at[step],
            ygot.at[step],
            device_id=y_peer(step),
            device_id_type=MESH,
        )

    send_top(0)
    for step in (4, 3, 5, 2, 6, 1, 7):
        entries = []
        for slot in range(CAP_Z):
            main = tab[0, step * CAP_Z + slot]
            entries.append((main, main + 2, None))
        move_records(own, entries, out_z.at[step], 0)
        z_copy(step).start()
    for tile in range(OWN):
        pool[tile] = own[tile]
    tops[1, 0] = take_top(0)
    send_top(1)
    tops[2, 0] = take_top(1)
    send_top(2)

    def records(first, count):
        return [tuple(tab[1 + part, first + slot] for part in range(3)) for slot in range(count)]

    for step in (1, 7, 2, 6, 3, 5, 4):
        z_copy(step).wait()
    for step in (2, 1, 3):
        move_records(pool, records((step - 1) * CAP_Y, CAP_Y), out_y.at[step], 0)
        y_copy(step).start()
    move_records(pool, records(3 * CAP_Y, CAP_HERE), got_ref, HERE)
    top_ref[...] = take_top(2)
    for step in (1, 3, 2):
        y_copy(step).wait()


def share(state, neighbours):
    vmem = pl.BlockSpec(memory_space=pltpu.VMEM)
    anywhere = pl.BlockSpec(memory_space=pl.ANY)
    return pl.pallas_call(
        share_kernel,
        out_shape=(
            jax.ShapeDtypeStruct((HERE + unit_tiles(CAP_HERE), 8, 128), jnp.float32),
            jax.ShapeDtypeStruct((2, 128), jnp.float32),
            jax.ShapeDtypeStruct((8, 128), jnp.int32),
        ),
        in_specs=[anywhere, anywhere],
        out_specs=(vmem, vmem, vmem),
        scratch_shapes=[
            pltpu.VMEM(state.shape, jnp.float32),
            pltpu.VMEM((2 * COLS_Z, 6), jnp.int32),
            pltpu.SMEM((8, 128), jnp.int32),
            pltpu.VMEM((OWN, 8, 128), jnp.float32),
            pltpu.VMEM((OWN + 7 * UNIT_Z, 8, 128), jnp.float32),
            pltpu.VMEM((COLS_Z, UNIT_Z, 8, 128), jnp.float32),
            pltpu.VMEM((ROWS_Y, UNIT_Y, 8, 128), jnp.float32),
            pltpu.VMEM((3, 8, 2, 128), jnp.float32),
            pltpu.SemaphoreType.DMA((3,)),
            pltpu.SemaphoreType.DMA((COLS_Z,)),
            pltpu.SemaphoreType.DMA((COLS_Z,)),
            pltpu.SemaphoreType.DMA((ROWS_Y,)),
            pltpu.SemaphoreType.DMA((ROWS_Y,)),
            pltpu.SemaphoreType.DMA((3, 8)),
            pltpu.SemaphoreType.DMA((3, 8)),
        ],
        compiler_params=pltpu.CompilerParams(
            collective_id=0, has_side_effects=True, vmem_limit_bytes=32 << 20
        ),
    )(state, neighbours)


def direct_kernel(base, table_ref, x_ref, got_ref, pool, out, ssem, rsem):
    group = lax.axis_index("group")
    dev = lax.axis_index("dev")
    barrier = pltpu.get_barrier_semaphore()

    def peer(step):
        return (group, lax.rem(dev + step, DEVS))

    def greet(step, carry):
        pl.semaphore_signal(barrier, inc=1, device_id=peer(step), device_id_type=MESH)
        return carry

    lax.fori_loop(1, DEVS, greet, 0)
    pack_faces(x_ref, pool)
    pl.semaphore_wait(barrier, DEVS - 1)

    def large(step):
        return pltpu.make_async_remote_copy(
            out.at[step],
            got_ref.at[step],
            ssem.at[step],
            rsem.at[step],
            device_id=peer(step),
            device_id_type=MESH,
        )

    def fill(step, target):
        entries = []
        for slot in (base, base + 1):
            main = table_ref[4 * step + slot] * RECORD
            entries.append((main, main + 2, None))
        move_records(pool, entries, target.at[step], 0)

    def send(step, carry):
        fill(step, out)
        large(step).start()
        return carry

    lax.fori_loop(1, DEVS, send, 0)
    fill(0, got_ref)

    def finish(step, carry):
        large(step).wait()
        return carry

    lax.fori_loop(1, DEVS, finish, 0)


def direct(table, state, base):
    vmem = pl.BlockSpec(memory_space=pltpu.VMEM)
    return pl.pallas_call(
        functools.partial(direct_kernel, base),
        out_shape=jax.ShapeDtypeStruct((DEVS, UNIT, 8, 128), jnp.float32),
        in_specs=[pl.BlockSpec(memory_space=pltpu.SMEM), vmem],
        out_specs=vmem,
        scratch_shapes=[
            pltpu.VMEM((OWN, 8, 128), jnp.float32),
            pltpu.VMEM((DEVS, UNIT, 8, 128), jnp.float32),
            pltpu.SemaphoreType.DMA((DEVS,)),
            pltpu.SemaphoreType.DMA((DEVS,)),
        ],
        compiler_params=pltpu.CompilerParams(
            collective_id=3 + base // 2, has_side_effects=True, vmem_limit_bytes=32 << 20
        ),
    )(table, state)


def rolled(arrays, amount, axis):
    return [pltpu.roll(a, amount % a.shape[axis], axis) for a in arrays]


def difference(states, normal, axis, unit):
    lefts, rights = [], []
    for field in states:
        (before,) = rolled([field], unit, axis)
        jump = field - before
        (after,) = rolled([jump], -unit, axis)
        half = 0.5 * minmod(jump, after)
        lefts.append(field + half)
        rights.append(field - half)
    fluxes = hll(rolled(lefts, unit, axis), rights, normal)
    return [high - low for high, low in zip(rolled(fluxes, -unit, axis), fluxes)]


def step_kernel(where_ref, owner_ref, x_ref, got_ref, top_ref, out_ref, turned_ref, total_ref, fresh, moved, ssem, rsem):
    group = lax.axis_index("group")
    dev = lax.axis_index("dev")
    parity = dev % 2
    partner = (group, dev + 1 - 2 * parity)
    border = 1 - parity
    barrier = pltpu.get_barrier_semaphore()
    pl.semaphore_signal(barrier, inc=1, device_id=partner, device_id_type=MESH)
    ratio = COURANT / jnp.max(top_ref[0:1, :], axis=(0, 1), keepdims=True)
    matrix = swap_matrix(PLANE, lambda layer: layer)
    lane = lanes(EDGE)
    half = lanes(8) < 64
    row8 = lax.broadcasted_iota(jnp.int32, (8, PLANE), 0)

    def fetch(box, face):
        spot = box * 6 + face
        main = where_ref[4, spot]
        main = jnp.concatenate([got_ref[main], got_ref[main + 1]], axis=0)
        extra = got_ref[where_ref[5, spot]]
        side = jnp.full((8, 128), where_ref[6, spot], jnp.int32)
        extra = jnp.where(side == 0, extra, pltpu.roll(extra, 64, 1))
        return main, extra, where_ref[7, spot]

    def lane_ghosts(main, extra, target):
        out = []
        for field in range(4):
            out.append(pltpu.roll(main, (target - 32 * field) % 128, 1))
        first = pltpu.roll(extra, target % 128, 1)
        second = pltpu.roll(extra, (target - 32) % 128, 1)
        out.append(jnp.concatenate([first, second], axis=0))
        return out

    def row_ghosts(main, extra):
        out = []
        last = jnp.where(half[0:4], extra[0:4], pltpu.roll(extra, 64, 1)[4:8])
        for field in range(FIELDS):
            rows = main[4 * field : 4 * field + 4] if field < 4 else last
            out.append(
                [
                    jnp.concatenate([rows[2 * layer : 2 * layer + 1], rows[2 * layer + 1 : 2 * layer + 2]], axis=1)
                    for layer in range(2)
                ]
            )
        return out

    copy = pltpu.make_async_remote_copy(
        fresh.at[border], moved, ssem, rsem, device_id=partner, device_id_type=MESH
    )

    def one_box(index, carry):
        box = lax.rem(border + index, 2)
        cells = [x_ref[box, field] for field in range(FIELDS)]
        turned_ref[...] = exact_permute(jnp.concatenate(cells, axis=0), matrix)
        low_main, low_extra, low_there = fetch(box, 0)
        high_main, high_extra, high_there = fetch(box, 1)
        low = row_ghosts(low_main, low_extra)
        high = row_ghosts(high_main, high_extra)
        low_there = jnp.full((1, PLANE), low_there, jnp.int32) > 0
        high_there = jnp.full((1, PLANE), high_there, jnp.int32) > 0
        extended = []
        for field in range(FIELDS):
            edge_low = cells[field][0:1]
            edge_high = cells[field][EDGE - 1 : EDGE]
            l0 = jnp.where(low_there, low[field][0], edge_low)
            l1 = jnp.where(low_there, low[field][1], edge_low)
            h0 = jnp.where(high_there, high[field][0], edge_high)
            h1 = jnp.where(high_there, high[field][1], edge_high)
            tile = jnp.where(row8 == 0, h0, jnp.where(row8 == 7, l1, jnp.where(row8 == 6, l0, h1)))
            extended.append(jnp.concatenate([cells[field], tile], axis=0))
        for part in range(2):
            states = primitive([e[:, 128 * part : 128 * part + 128] for e in extended])
            parts = difference(states, 0, 0, 1)
            for field in range(FIELDS):
                total_ref[field, :, 128 * part : 128 * part + 128] = parts[field][0:EDGE]
        for axis in (2, 1):
            if axis == 1:
                source = cells
            else:
                source = [turned_ref[EDGE * f : EDGE * f + EDGE] for f in range(FIELDS)]
            low_main, low_extra, low_there = fetch(box, 2 * axis)
            high_main, high_extra, high_there = fetch(box, 2 * axis + 1)
            there = jnp.where(lane < 64, jnp.full((EDGE, 128), high_there, jnp.int32), low_there) > 0
            low = lane_ghosts(low_main, low_extra, 96)
            high = lane_ghosts(high_main, high_extra, 0)
            extended = []
            for field in range(FIELDS):
                left, right = source[field][:, 0:128], source[field][:, 128:256]
                edge_low = jnp.where(lane < 112, pltpu.roll(left, 96, 1), pltpu.roll(left, 112, 1))
                edge_high = jnp.where(lane < 16, pltpu.roll(right, 16, 1), pltpu.roll(right, 32, 1))
                ghost = jnp.where(lane < 64, high[field], low[field])
                tile = jnp.where(there, ghost, jnp.where(lane < 64, edge_high, edge_low))
                extended.append(jnp.concatenate([left, right, tile], axis=1))
            pieces = []
            for part in range(2):
                states = primitive([e[8 * part : 8 * part + 8] for e in extended])
                pieces.append(difference(states, axis, 1, EDGE))
            if axis == 2:
                stacked = jnp.concatenate(
                    [pieces[part][f][:, 0:PLANE] for f in range(FIELDS) for part in range(2)], axis=0
                )
                turned_ref[...] = exact_permute(stacked, matrix)
            else:
                for field in range(FIELDS):
                    along = jnp.concatenate([pieces[part][field][:, 0:PLANE] for part in range(2)], axis=0)
                    total = (total_ref[field] + along) + turned_ref[EDGE * field : EDGE * field + EDGE]
                    fresh[box, field] = cells[field] - ratio * total

        @pl.when(index == 0)
        def _():
            pl.semaphore_wait(barrier, 1)
            copy.start()

        return carry

    lax.fori_loop(0, 2, one_box, 0)
    copy.wait()
    pair = (group * DEVS + dev) // 2
    split = jnp.zeros((EDGE, PLANE), jnp.int32)
    for box in range(4):
        split = split + jnp.where(jnp.full((EDGE, PLANE), owner_ref[4 * pair + box], jnp.int32) == 2 * pair, 1, 0)
    lower = jnp.full((EDGE, PLANE), parity, jnp.int32) == 0
    for field in range(FIELDS):
        zero, one, other = fresh[0, field], fresh[1, field], moved[field]
        none = jnp.zeros_like(zero)
        early = jnp.where(split == 1, other, jnp.where(split == 2, zero, one))
        out_ref[0, field] = jnp.where(lower, zero, early)
        low = jnp.where(split >= 2, one, none)
        high = jnp.where(split == 1, zero, jnp.where(split == 2, one, none))
        out_ref[1, field] = jnp.where(lower, low, high)
        low = jnp.where(split == 3, other, none)
        high = jnp.where(split == 1, one, none)
        out_ref[2, field] = jnp.where(lower, low, high)


def advance(where, new_owner, state, got, top, number):
    vmem = pl.BlockSpec(memory_space=pltpu.VMEM)
    box = state.shape[1:]
    return pl.pallas_call(
        step_kernel,
        out_shape=jax.ShapeDtypeStruct((3,) + box, state.dtype),
        in_specs=[pl.BlockSpec(memory_space=pltpu.SMEM)] * 2 + [vmem] * 3,
        out_specs=vmem,
        scratch_shapes=[
            pltpu.VMEM((FIELDS * EDGE, PLANE), jnp.float32),
            pltpu.VMEM((FIELDS, EDGE, PLANE), jnp.float32),
            pltpu.VMEM((2,) + box, jnp.float32),
            pltpu.VMEM(box, jnp.float32),
            pltpu.SemaphoreType.DMA,
            pltpu.SemaphoreType.DMA,
        ],
        compiler_params=pltpu.CompilerParams(
            collective_id=number, has_side_effects=True, vmem_limit_bytes=32 << 20
        ),
    )(where, new_owner, state, got, top)


def count(test, axis):
    return jnp.sum(test.astype(jnp.int32), axis=axis)


def direct_tables(near, dev):
    face = jnp.arange(FACES, dtype=jnp.int32)
    there = near >= 0
    other = jnp.where(there, (near // 2) % DEVS, -1)
    same = (other[:, None] == other[None, :]) & there[:, None] & there[None, :]
    rank = count(same & (face[None, :] < face[:, None]), 1)
    far_face = (near % 2) * 6 + ((face % 6) ^ 1)
    far_rank = count(same & (far_face[None, :] < far_face[:, None]), 1)
    place = jnp.where(there, ((other - dev + DEVS) % DEVS) * 4 + rank, -1)
    spot = jnp.arange(4 * DEVS, dtype=jnp.int32)
    hit = spot[:, None] == place[None, :]
    table = FACES + jnp.sum(jnp.where(hit, face[None, :] - FACES, 0), axis=1)
    begin = (((dev - other + DEVS) % DEVS) * 2 + far_rank // 2) * UNIT
    where = jnp.stack([begin + 2 * (far_rank % 2), begin + 4, far_rank % 2, jnp.ones_like(near)])
    return table, jnp.pad(jnp.where(there, where, 0), ((4, 0), (0, 128 - FACES)))


def body(state, new_owner, neighbours):
    group = lax.axis_index("group")
    dev = lax.axis_index("dev")
    got, top, where = share(state, neighbours)

    def fits(state):
        return advance(where, new_owner, state, got, top, 1)

    def crowded(state):
        near = lax.dynamic_slice_in_dim(neighbours, 2 * (group * DEVS + dev), 2, 0).reshape(FACES)
        table, where = direct_tables(near, dev)
        both = jnp.concatenate([direct(table, state, 0), direct(table, state, 2)], axis=1)
        return advance(where, new_owner, state, both.reshape(-1, 8, 128), top, 2)

    return lax.cond(top[1, 0] > 0.5, crowded, fits, state)


def solution(mesh):
    placed = (P(("group", "dev"), None, None, None), P(), P())
    return jax.shard_map(
        body,
        mesh=mesh,
        in_specs=placed,
        out_specs=P(("group", "dev"), None, None, None),
        check_vma=False,
    )
```

time: 69.1 us -> 34.5 us (0.50); the launches traced: 68 us -> 34.2 us
  Pallas kernels: 55.1 us -> 31.5 us
  other arithmetic: 4.4 us -> 0 us
  between operations: 3.24 us -> 0.68 us
  local copies, waits for them, and re-layouts: 4.54 us -> 2.06 us
  starting transfers between devices: 0.7 us -> 0 us
    pallas_call x3 -> x2, Pallas kernels: 55.1 us -> 31.5 us  [the longest x1 24.9 us: share(): pl.pallas_call(share_kernel, out_shape=(jax.ShapeDtypeStruct((HERE + unit...]
    cond x2 -> x0, local copies, waits for them, and re-layouts: 1.77 us -> none
    reduce_sum x4 -> x0, other arithmetic: 1.74 us -> none  [the longest x1 1.4 us: body(): split = jnp.sum((owners == place // 2 * 2).astype(jnp.int32))]
    select_n x4 -> x0, other arithmetic: 1.01 us -> none  [the longest x1 0.95 us: body(): pick = lambda test, a, b: jnp.where(test, a, b)]
    dynamic_slice x2 -> x0, local copies, waits for them, and re-layouts: 0.89 us -> none  [body(): near = lax.dynamic_slice_in_dim(neighbours, 2 * place, 2, 0).reshape(FACES)]
    another operation x2 -> x0, other arithmetic: 0.73 us -> none  [body(): return jnp.stack([pick(parity == 0, a, b) for a, b in zip(even, odd)])]
    ppermute x1 -> x0, starting transfers between devices: 0.7 us -> none  [body(): lax.ppermute(jnp.where(parity == 0, fresh[1], fresh[0]), 'dev', route)]
    unnamed x3 -> x2, local copies, waits for them, and re-layouts: 0.86 us -> 1.55 us
  transfers between devices with their start and end apart: 1 -> 0, of which waited for: 0 -> 0; matrix products, arithmetic and copies ran while one was open for 3% -> 0% of each run, Pallas kernels for 0% -> 0%
where the time goes in v2:
time: 34.5 us; the launch traced here: 34.2 us
  Pallas kernels  31.5 us (91%)
  local copies, waits for them, and re-layouts  2.06 us (6%)
  between operations  0.68 us (2%)
    pallas_call x1, Pallas kernels, share(): pl.pallas_call(share_kernel, out_shape=(jax.ShapeDtypeStruct((HERE + unit...  24.9 us
    pallas_call x1, Pallas kernels, advance(): pl.pallas_call(step_kernel, out_shape=jax.ShapeDtypeStruct((3,) + box, st...  6.56 us
    unnamed x2, local copies, waits for them, and re-layouts  1.55 us

profile of v2, /device:TPU:32, one launch (start us, length us, event | category | flops | bytes accessed | tf_op | source)
XLA Modules:
  0.0 34.2 jit_solution(9016659652417386501)
XLA Ops:
  0.0 0.9 %copy.8.near_hbm = s32[512,6]{1,0:T(8,128)S(1)} copy(s32[512,6]{0,1:T(8,128)} %param.7) | data formatting | bytes 24576 | tf_op args[2]
  0.9 24.9 %shard_map.39 = (f32[75,8,128]{2,1,0:T(8,128)S(1)}, f32[2,128]{1,0:T(2,128)S(1)}, s32[8,128]{1,0:T(8,128)S(1)}) custom-call(f32[2,5,16,256]{3,2,1,0:T(8,128)} %x_hbm.1, s32[512,6]{1,0:T(8,128)S(1)} %copy.8.near_hbm), custom_call_target="tpu_custom_call" | custom-call | tf_op jit(solution)/shard_map/pallas_call | solution.py:365
  25.8 0.5 %slice.3 = f32[1,1]{1,0:T(1,128)} slice(f32[2,128]{1,0:T(2,128)S(1)} %get-tuple-element.44), slice={[1:2], [0:1]} | slice | bytes 8 | tf_op jit(solution)/shard_map/slice | solution.py:672
  26.9 6.6 %conditional.1 = (f32[3,5,16,256]{3,2,1,0:T(8,128)S(1)}) conditional(s32[]{:T(128)} %bitcast.2, (s32[8,128]{1,0:T(8,128)S(1)}, s32[512]{0:T(512)}, f32[2,5,16,256]{3,2,1,0:T(8,128)}, f32[75,8,128]{2,1,0:T(8,128)S(1)}, f32[2,128]{1,0:T(2,128)S(1)}) %tuple.11, (s32[]{:T(128)}, s32[]{:T(128)}, s32[512,6]{0,1:T(8,128)}, f32[2,5,16,256]{3,2,1,0:T(8,128)}, ...), branch_computations={%region_0.0_spmd, %region_1.5_spmd} | conditional | flops 335558 | bytes 3317358 | solution.py:672
  27.0 6.6 %branch_0_fun.1 = f32[3,5,16,256]{3,2,1,0:T(8,128)S(1)} custom-call(s32[8,128]{1,0:T(8,128)S(1)} %get-tuple-element.30.where_ref, s32[512]{0:T(512)} %get-tuple-element.31.owner_ref, f32[2,5,16,256]{3,2,1,0:T(8,128)} %get-tuple-element.32.x_ref, f32[75,8,128]{2,1,0:T(8,128)S(1)} %get-tuple-element.33.got_ref, f32[2,128]{1,0:T(2,128)S(1)} %get-tuple-element.34.top_ref), custom_call_target="tpu_custom_call" | custom-call | tf_op jit(solution)/shard_map/cond/branch_0_fun/pallas_call | solution.py:618
  33.5 0.7 %copy.13 = f32[3,5,16,256]{3,2,1,0:T(8,128)} copy(f32[3,5,16,256]{3,2,1,0:T(8,128)S(1)} %get-tuple-element.47) | data formatting | bytes 491520
